TPU v7x, 512 devices: a whole 4x4x16 slice. The times are simulated.
512 devices in a mesh: cube: 128 (over z, y, core), front: 4 (over x).
Axes of the slice: x: 4, y: 4, z: 16, core: 2. Of those that a mesh axis runs over, the one named last changes fastest.
Arguments:
- kkt_blocks: float32 [4, 32768, 128], P('front', 'cube'), may hold values from -1.5 to 1.5
- kkt_owner: int32 [4, 32768, 1], P('front', 'cube'), may hold values from 0 to 127; in each aligned block of 256 rows (0 to 255, 256 to 511, ..., all dimensions but the last counted through in order) at most 4 rows name the same one
- kkt_target: int32 [4, 32768], P('front', 'cube'), may hold values from 0 to 255
- leaf_pivot: float32 [256, 512, 128], P('cube', 'front'), may hold values from -3.5 to 3.5
- pivot_signs: int32 [256, 512], P('cube', 'front'), may hold values from -1 to 1, as said below
- perturb: float32 [256, 512], P('cube', 'front'), may hold values from 0.25 to 1
- leaf_coupling: float32 [256, 512, 128], P('cube', 'front'), may hold values from -1.5 to 1.5
- leaf_map: int32 [256, 512], P('cube', 'front'), may hold values from 256 to 2047
- mid_front: bfloat16 [131072, 2048], P('cube', 'front'), may hold values from -3.5 to 3.5
- level_map: int32 [64, 2048], replicated, may hold values from 256 to 2047, as said below
- top_front: bfloat16 [65536, 2048], P('cube', 'front'), may hold values from -3.5 to 3.5
Outputs:
- leaf_factor: float32 [256, 512, 128], P('cube', 'front')
- mid_factor: float32 [131072, 256], P(('cube', 'front'))
- upper_schur: float32 [65536, 2048], P('cube', 'front')
Inputs may be any that keep to these rules, and one draw needn't show every extreme that they name: `kkt_owner`: the rows of one device name one cube index at most 4 times, and some cube index exactly 4 times. `pivot_signs`: every entry is -1 or 1. `level_map`: position p of a level-1 front goes to a position of the same quarter floor(p / 512) of the level-2 front, never below 256.
All inputs are finite; a program needn't handle non-finite values.
Results may differ from a plain program's by a relative error of at most 0.0003.
Values sent between devices are 32-bit elements; how exact they have to be, the bound alone decides.
A program may use at most 64 MiB of HBM per device.

v0:
```python
import jax
import jax.numpy as jnp
from jax import lax
from jax.sharding import PartitionSpec as P

NU = 2048
PIV = 128
PANELS = 2
NS_STEPS = 2


HIGHEST = lax.Precision.HIGHEST


def partner(array, axis, stride):
    return lax.ppermute(array, axis, [(i, i ^ 1 << stride) for i in range(lax.axis_size(axis))])


def from_root(array, axis, root):
    mine = lax.axis_index(axis) == root
    return lax.psum(jnp.where(mine, array, jnp.zeros_like(array)), axis)


def newton_inverse(pivot_block):
    diagonal = jnp.diagonal(pivot_block, axis1=-2, axis2=-1)
    current = jnp.eye(pivot_block.shape[-1], dtype=jnp.float32) * (1.0 / diagonal)[..., None, :]
    for sweep_index in range(NS_STEPS):
        product = jnp.einsum("...ij,...jk->...ik", pivot_block, current, precision=HIGHEST)
        current = 2.0 * current - jnp.einsum(
            "...ij,...jk->...ik", current, product, precision=HIGHEST
        )
    return current


def apply_panel(front_block, own_cols, pivot_rows, col_rows, row_positions, col_positions, finish):
    inverse = newton_inverse(pivot_rows)
    keep_rows = (row_positions >= finish).astype(jnp.float32)[:, None]
    keep_cols = (col_positions >= finish).astype(jnp.float32)[:, None]
    lower_rows = jnp.dot(own_cols, inverse, precision=HIGHEST) * keep_rows
    return (
        front_block - jnp.dot(lower_rows, (col_rows * keep_cols).T, precision=HIGHEST),
        lower_rows,
    )


def local(
    kkt_blocks,
    kkt_owner,
    kkt_target,
    leaf_pivot,
    pivot_signs,
    perturb,
    leaf_coupling,
    leaf_map,
    mid_front,
    level_map,
    top_front,
):
    cube_count = lax.axis_size("cube")
    front_count = lax.axis_size("front")
    cube_pos = lax.axis_index("cube")
    front_pos = lax.axis_index("front")
    low_bit = cube_pos % 2
    high_bit = cube_pos // 2 % 2
    blocks = kkt_blocks[0]
    block_count = blocks.shape[0]
    block_width = blocks.shape[1]
    capacity = max(2, 2 * block_count // cube_count)
    destination = kkt_owner[0, :, 0]
    onehot = (destination[:, None] == jnp.arange(cube_count, dtype=jnp.int32)[None, :]).astype(
        jnp.int32
    )
    slot_rank = jnp.sum((jnp.cumsum(onehot, axis=0) - 1) * onehot, axis=1)
    send_slot = destination * capacity + slot_rank
    send_values = (
        jnp.zeros((cube_count * capacity, block_width), jnp.float32).at[send_slot].set(blocks)
    )
    send_rows = (
        jnp.full((cube_count * capacity,), -1.0, jnp.float32)
        .at[send_slot]
        .set(kkt_target[0].astype(jnp.float32))
    )
    got_values, got_rows = (
        lax.all_to_all(
            send_values.reshape(cube_count, capacity, block_width),
            "cube",
            split_axis=0,
            concat_axis=0,
            tiled=True,
        ),
        lax.all_to_all(
            send_rows.reshape(cube_count, capacity), "cube", split_axis=0, concat_axis=0, tiled=True
        ),
    )
    leaf_count = leaf_pivot.shape[0]
    pivot_size = leaf_pivot.shape[2]
    row_count = leaf_coupling.shape[1]
    identity = jnp.eye(pivot_size, dtype=jnp.float32)
    pivots = leaf_pivot + identity * (pivot_signs.astype(jnp.float32) * perturb)[:, None, :]
    inverse = newton_inverse(pivots)
    leaf_rows = leaf_count * row_count
    targets = got_rows.reshape(-1).astype(jnp.int32)
    targets = jnp.where(targets < 0, leaf_rows, targets)
    arrivals = jax.ops.segment_sum(
        got_values.reshape(-1, block_width), targets, num_segments=leaf_rows + 1
    )[:leaf_rows]
    coupling = leaf_coupling + arrivals.reshape(leaf_count, row_count, block_width)
    factor = jnp.einsum("lrk,lkj->lrj", coupling, inverse, precision=HIGHEST)
    contrib = -jnp.einsum("lrk,lsk->lrs", factor, coupling, precision=HIGHEST)
    shared_terms, shared_maps = (
        lax.all_gather(contrib, "front", axis=0, tiled=True),
        lax.all_gather(leaf_map.astype(jnp.float32), "front", axis=0, tiled=True),
    )
    partner_terms, partner_maps = partner((shared_terms, shared_maps), "cube", 0)
    child_terms = jnp.concatenate([shared_terms, partner_terms], axis=0)
    child_maps = jnp.concatenate([shared_maps, partner_maps], axis=0).astype(jnp.int32)
    half_rows = NU // 2
    quarter = NU // 4
    child_count = child_terms.shape[0]
    child_rows = child_terms.shape[1]
    row_local = child_maps - low_bit * half_rows
    col_local = child_maps - front_pos * quarter
    row_valid = (row_local >= 0) & (row_local < half_rows)
    col_valid = (col_local >= 0) & (col_local < quarter)
    block_ids = jnp.arange(child_count, dtype=jnp.int32)[:, None]
    col_ids = jnp.where(col_valid, block_ids * quarter + col_local, child_count * quarter)
    by_cols = jax.ops.segment_sum(
        jnp.swapaxes(child_terms, 1, 2).reshape(-1, child_rows),
        col_ids.reshape(-1),
        num_segments=child_count * quarter + 1,
    )[:-1]
    by_cols = jnp.swapaxes(by_cols.reshape(child_count, quarter, child_rows), 1, 2).reshape(
        -1, quarter
    )
    row_ids = jnp.where(row_valid, row_local, half_rows)
    assembled = jax.ops.segment_sum(by_cols, row_ids.reshape(-1), num_segments=half_rows + 1)[:-1]
    mid_block = mid_front.astype(jnp.float32) + assembled
    mid_positions = low_bit * half_rows + jnp.arange(half_rows)
    col_positions = front_pos * quarter + jnp.arange(quarter)
    factors = []
    for panel_index in range(PANELS):
        first_col = panel_index * PIV
        finish = first_col + PIV
        own_cols = from_root(mid_block[:, first_col:finish], "front", 0)
        other_cols = partner(own_cols, "cube", 0)
        whole_cols = jnp.where(
            low_bit == 0,
            jnp.concatenate([own_cols, other_cols], axis=0),
            jnp.concatenate([other_cols, own_cols], axis=0),
        )
        pivot_rows = whole_cols[first_col:finish]
        col_rows = lax.dynamic_slice_in_dim(whole_cols, front_pos * quarter, quarter, 0)
        mid_block, lower_rows = apply_panel(
            mid_block, own_cols, pivot_rows, col_rows, mid_positions, col_positions, finish
        )
        factors.append(lower_rows)
    factor_rows = jnp.concatenate(factors, axis=1)
    slab_rows = half_rows // front_count
    mid_factor = lax.dynamic_slice_in_dim(factor_rows, front_pos * slab_rows, slab_rows, 0)
    group_one = cube_pos // 2
    other_group = group_one + 1 - 2 * high_bit
    own_map = lax.dynamic_index_in_dim(level_map, group_one, 0, keepdims=False)
    other_map = lax.dynamic_index_in_dim(level_map, other_group, 0, keepdims=False)
    own_piece = lax.dynamic_slice_in_dim(mid_block, high_bit * quarter, quarter, 0)
    received = partner(mid_block, "cube", 1)
    other_piece = lax.dynamic_slice_in_dim(received, high_bit * quarter, quarter, 0)
    row_quarter = 2 * low_bit + high_bit
    top_positions = row_quarter * quarter + jnp.arange(quarter)

    def spread_cols(piece, mapping):
        col_target = jnp.take(mapping, col_positions) - front_pos * quarter
        col_ids = jnp.where(col_positions >= PANELS * PIV, col_target, quarter)
        return jax.ops.segment_sum(piece.T, col_ids, num_segments=quarter + 1)[:-1].T

    def row_ids_of(mapping):
        row_target = jnp.take(mapping, top_positions) - row_quarter * quarter
        return jnp.where(top_positions >= PANELS * PIV, row_target, quarter)

    top_rows = jnp.concatenate(
        [spread_cols(own_piece, own_map), spread_cols(other_piece, other_map)], axis=0
    )
    top_ids = jnp.concatenate([row_ids_of(own_map), row_ids_of(other_map)])
    top_added = jax.ops.segment_sum(top_rows, top_ids, num_segments=quarter + 1)[:-1]
    top_block = top_front.astype(jnp.float32) + top_added
    for panel_index in range(PANELS):
        first_col = panel_index * PIV
        finish = first_col + PIV
        own_cols = from_root(top_block[:, first_col:finish], "front", 0)
        first_swap = partner(own_cols, "cube", 0)
        by_low = jnp.where(
            low_bit == 0, jnp.stack([own_cols, first_swap]), jnp.stack([first_swap, own_cols])
        )
        second_swap = partner(by_low, "cube", 1)
        by_both = jnp.where(
            high_bit == 0,
            jnp.stack([by_low, second_swap], axis=1),
            jnp.stack([second_swap, by_low], axis=1),
        )
        whole_cols = by_both.reshape(NU, PIV)
        pivot_rows = whole_cols[first_col:finish]
        col_rows = lax.dynamic_slice_in_dim(whole_cols, front_pos * quarter, quarter, 0)
        top_block, unused = apply_panel(
            top_block, own_cols, pivot_rows, col_rows, top_positions, col_positions, finish
        )
    return (factor, mid_factor, top_block)


def solution(mesh):
    in_specs = (
        P("front", "cube", None),
        P("front", "cube", None),
        P("front", "cube"),
        P("cube", "front", None),
        P("cube", "front"),
        P("cube", "front"),
        P("cube", "front", None),
        P("cube", "front"),
        P("cube", "front"),
        P(),
        P("cube", "front"),
    )
    out_specs = (P("cube", "front", None), P(("cube", "front"), None), P("cube", "front"))
    return jax.shard_map(local, mesh=mesh, in_specs=in_specs, out_specs=out_specs, check_vma=False)
```

profile of v0, /device:TPU:1, one launch (start us, length us, event | category | flops | bytes accessed | tf_op | source)
XLA Modules:
  0.0 541.4 jit_solution(2632494190466189696)
XLA Ops:
  7.9 8.5 %all-gather = f32[4,2,128]{2,1,0:T(2,128)S(1)} all-gather(f32[1,2,128]{2,1,0:T(2,128)S(1)} %convert_bitcast_fusion), channel_id=1, replica_groups=mesh['cube'=128,'front'=4] {'front'}, dimensions={0}, use_global_device_ids=true | all-gather | bytes 5120 | tf_op jit(solution)/shard_map/all_gather | solution.py:112
  16.4 7.2 %collective-permute-start = (f32[8,128]{1,0:T(8,128)S(1)}, f32[8,128]{1,0:T(8,128)S(1)}, u32[]{:S(2)}, u32[]{:S(2)}) collective-permute-start(f32[8,128]{1,0:T(8,128)S(1)} %bitcast.138), channel_id=1, source_target_pairs={{0,4},{4,0},{8,12},{12,8},{16,20},{20,16},{24,28},{28,24},{32,36},... | collective-permute-start | bytes 12296 | tf_op jit(solution)/shard_map/ppermute | solution.py:16
  29.1 16.5 %all-to-all-start = ((f32[128,1,4]{2,1,0:T(1,128)}), f32[128,1,4]{2,1,0:T(1,128)S(1)}, u32[]{:S(2)}, u32[]{:S(2)}) async-start(f32[128,1,4]{2,1,0:T(1,128)} %bitcast.9), calls=%async_computation | async-start | bytes 131072 | tf_op jit(solution)/shard_map/all_to_all | solution.py:91
  47.4 4.6 copy.44
  56.0 4.5 all-to-all-done
  60.5 11.6 %all-to-all-start.1 = ((f32[128,4,128]{2,1,0:T(4,128)}), f32[128,4,128]{2,1,0:T(4,128)S(1)}, u32[]{:S(2)}, u32[]{:S(2)}) async-start(f32[128,4,128]{2,1,0:T(4,128)} %bitcast.12), calls=%async_computation.1 | async-start | bytes 524288 | tf_op jit(solution)/shard_map/all_to_all | solution.py:84
  73.3 19.3 %all-to-all-done.1 = f32[128,4,128]{2,1,0:T(4,128)S(1)} async-done(((f32[128,4,128]{2,1,0:T(4,128)}), f32[128,4,128]{2,1,0:T(4,128)S(1)}, u32[]{:S(2)}, u32[]{:S(2)}) %all-to-all-start.1) | async-done | bytes 262176 | tf_op jit(solution)/shard_map/all_to_all | solution.py:84
  92.6 3.2 scatter_custom_fusion.2
  96.6 11.1 %all_gather.7 = f32[8,128,128]{2,1,0:T(8,128)S(1)} all-gather(f32[2,128,128]{2,1,0:T(8,128)S(1)} %convolution_negate_fusion), channel_id=1, replica_groups=mesh['cube'=128,'front'=4] {'front'}, dimensions={0}, use_global_device_ids=true | all-gather | bytes 655360 | tf_op jit(solution)/shard_map/all_gather | solution.py:111
  107.8 4.3 collective-permute-start.1
  113.3 15.0 %scatter_custom_fusion.3 = f32[8193,128]{1,0:T(8,128)} fusion(s32[2048]{0:T(1024)S(1)} %get-tuple-element.15, f32[2048,128]{1,0:T(8,128)S(1)} %bitcast.129, f32[]{:T(128)} %constant.62.clone.1), kind=kCustom, calls=%fused_computation.17 | custom fusion | flops 262144 | bytes 4194820 | tf_op jit(solution)/shard_map/scatter-add | solution.py:127
  128.3 4.4 slice.84
  132.7 5.3 copy.48
  138.1 13.8 %scatter_custom_fusion.4 = f32[1025,512]{1,0:T(8,128)S(1)} fusion(s32[2048]{0:T(1024)S(1)} %bitcast.142, f32[2048,512]{1,0:T(8,128)} %bitcast.114, f32[]{:T(128)} %constant.62.clone.1), kind=kCustom, calls=%fused_computation.43 | custom fusion | flops 1048576 | bytes 2099712 | tf_op jit(solution)/shard_map/scatter-add | solution.py:136
  154.5 46.7 %all-reduce.5.cloned.1.call-done = f32[1024,128]{1,0:T(8,128)} async-done(((f32[1024,128]{1,0:T(8,128)}), f32[1024,128]{1,0:T(8,128)}) %all-reduce.5.cloned.1.call-update) | async-done | bytes 524304 | tf_op jit(solution)/shard_map/psum | solution.py:21
  201.2 4.8 collective-permute-start.2
  211.9 3.7 convolution_subtract_fusion.1
  216.5 56.8 %all-reduce.7.cloned.1.call-done = f32[1024,128]{1,0:T(8,128)} async-done(((f32[1024,128]{1,0:T(8,128)}), f32[1024,128]{1,0:T(8,128)}) %all-reduce.7.cloned.1.call-update) | async-done | bytes 524304 | tf_op jit(solution)/shard_map/psum | solution.py:21
  273.3 4.9 collective-permute-start.3
  287.5 4.3 convolution_subtract_fusion
  295.9 3.1 gather_fusion.7
  299.0 3.1 gather_fusion.8
  311.2 5.0 scatter_custom_fusion.5
  319.7 21.1 %collective-permute-done.4 = f32[1024,512]{1,0:T(8,128)} collective-permute-done((f32[1024,512]{1,0:T(8,128)}, f32[1024,512]{1,0:T(8,128)}, u32[]{:S(2)}, u32[]{:S(2)}) %collective-permute-start.4) | collective-permute-done | bytes 2097184 | tf_op jit(solution)/shard_map/ppermute | solution.py:16
  343.4 4.7 scatter_custom_fusion.6
  350.9 7.9 %scatter_custom_fusion.7 = f32[513,512]{1,0:T(8,128)} fusion(s32[1024]{0:T(1024)S(1)} %pad_add_fusion, f32[512,512]{1,0:T(8,128)S(1)} %bitcast.116, f32[]{:T(128)} %constant.197, f32[512,512]{1,0:T(8,128)S(1)} %bitcast.115, f32[]{:T(128)} %constant.62.clone.1), kind=kCustom, calls=%fused_computation.20 | custom fusion | flops 1048576 | bytes 3147784 | tf_op jit(solution)/shard_map/scatter-add | solution.py:183
  361.1 56.6 %all-reduce.9.cloned.1.call-done = f32[512,128]{1,0:T(8,128)} async-done(((f32[512,128]{1,0:T(8,128)}), f32[512,128]{1,0:T(8,128)}) %all-reduce.9.cloned.1.call-update) | async-done | bytes 262160 | tf_op jit(solution)/shard_map/psum | solution.py:21
  417.7 4.7 collective-permute-start.5
  429.9 11.0 %collective-permute-done.6 = f32[2,512,128]{2,1,0:T(8,128)S(1)} collective-permute-done((f32[2,512,128]{2,1,0:T(8,128)}, f32[2,512,128]{2,1,0:T(8,128)S(1)}, u32[]{:S(2)}, u32[]{:S(2)}) %collective-permute-start.6) | collective-permute-done | bytes 524320 | tf_op jit(solution)/shard_map/ppermute | solution.py:16
  449.0 56.2 %all-reduce.11.cloned.1.call-done = f32[512,128]{1,0:T(8,128)} async-done(((f32[512,128]{1,0:T(8,128)}), f32[512,128]{1,0:T(8,128)}) %all-reduce.11.cloned.1.call-update) | async-done | bytes 262160 | tf_op jit(solution)/shard_map/psum | solution.py:21
  505.2 4.8 collective-permute-start.7
  517.3 11.3 %collective-permute-done.8 = f32[2,512,128]{2,1,0:T(8,128)} collective-permute-done((f32[2,512,128]{2,1,0:T(8,128)}, f32[2,512,128]{2,1,0:T(8,128)}, u32[]{:S(2)}, u32[]{:S(2)}) %collective-permute-start.8) | collective-permute-done | bytes 524320 | tf_op jit(solution)/shard_map/ppermute | solution.py:16
  (156 shorter events, 86.3 us)
Async XLA Ops:
  7.2 47.0 %copy-start = (f32[1,256,128]{2,1,0:T(8,128)S(1)}, f32[1,256,128]{2,1,0:T(8,128)}, u32[]{:S(2)}) copy-start(f32[1,256,128]{2,1,0:T(8,128)} %param.13) | copy-start | bytes 393220
  16.4 95.8 %collective-permute-start = (f32[8,128]{1,0:T(8,128)S(1)}, f32[8,128]{1,0:T(8,128)S(1)}, u32[]{:S(2)}, u32[]{:S(2)}) collective-permute-start(f32[8,128]{1,0:T(8,128)S(1)} %bitcast.138), channel_id=1, source_target_pairs={{0,4},{4,0},{8,12},{12,8},{16,20},{20,16},{24,28},{28,24},{32,36},... | collective-permute-start | bytes 12296 | tf_op jit(solution)/shard_map/ppermute | solution.py:16
  29.1 31.4 %all-to-all-start = ((f32[128,1,4]{2,1,0:T(1,128)}), f32[128,1,4]{2,1,0:T(1,128)S(1)}, u32[]{:S(2)}, u32[]{:S(2)}) async-start(f32[128,1,4]{2,1,0:T(1,128)} %bitcast.9), calls=%async_computation | async-start | bytes 131072 | tf_op jit(solution)/shard_map/all_to_all | solution.py:91
  52.0 43.9 %copy-start.12 = (f32[2,128,128]{2,1,0:T(8,128)S(1)}, f32[2,128,128]{2,1,0:T(8,128)}, u32[]{:S(2)}) copy-start(f32[2,128,128]{2,1,0:T(8,128)} %param.19) | copy-start | bytes 393220
  60.5 32.1 %all-to-all-start.1 = ((f32[128,4,128]{2,1,0:T(4,128)}), f32[128,4,128]{2,1,0:T(4,128)S(1)}, u32[]{:S(2)}, u32[]{:S(2)}) async-start(f32[128,4,128]{2,1,0:T(4,128)} %bitcast.12), calls=%async_computation.1 | async-start | bytes 524288 | tf_op jit(solution)/shard_map/all_to_all | solution.py:84
  72.1 129.1 %all-reduce.5.cloned.1.call-start = ((), (), s32[]{:S(2)}) async-start(), calls=%async_computation.2 | async-start | bytes 1048576 | tf_op jit(solution)/shard_map/psum | solution.py:21
  96.2 17.2 %copy-start.11 = (f32[2,128,128]{2,1,0:T(8,128)}, f32[2,128,128]{2,1,0:T(8,128)S(1)}, u32[]{:S(2)}) copy-start(f32[2,128,128]{2,1,0:T(8,128)S(1)} %fusion.116) | copy-start | bytes 393220
  107.8 5.4 collective-permute-start.1
  138.1 13.8 %copy-start.10 = (bf16[1024,512]{1,0:T(8,128)(2,1)S(1)}, bf16[1024,512]{1,0:T(8,128)(2,1)}, u32[]{:S(2)}) copy-start(bf16[1024,512]{1,0:T(8,128)(2,1)} %param.21) | copy-start | bytes 3145732
  152.2 1.4 copy-start.2
  154.4 118.9 %all-reduce.7.cloned.1.call-start = ((), (), s32[]{:S(2)}) async-start(), calls=%async_computation.3 | async-start | bytes 1048576 | tf_op jit(solution)/shard_map/psum | solution.py:21
  201.2 10.1 %copy-start.9 = (f32[1024,128]{1,0:T(8,128)S(1)}, f32[1024,128]{1,0:T(8,128)}, u32[]{:S(2)}) copy-start(f32[1024,128]{1,0:T(8,128)} %all-reduce.5.cloned.1.call-done) | copy-start | bytes 1572868
  201.2 6.6 %collective-permute-start.2 = (f32[1024,128]{1,0:T(8,128)}, f32[1024,128]{1,0:T(8,128)S(1)}, u32[]{:S(2)}, u32[]{:S(2)}) collective-permute-start(f32[1024,128]{1,0:T(8,128)} %all-reduce.5.cloned.1.call-done), channel_id=1, source_target_pairs={{0,4},{4,0},{8,12},{12,8},{16,20},{20,16},{24,28},{28,24},{32,36},... | collective-permute-start | bytes 1572872 | tf_op jit(solution)/shard_map/ppermute | solution.py:16
  209.1 2.1 copy-start.6
  216.5 201.2 %all-reduce.9.cloned.1.call-start = ((), (), s32[]{:S(2)}) async-start(), calls=%async_computation.4 | async-start | bytes 524288 | tf_op jit(solution)/shard_map/psum | solution.py:21
  273.3 6.4 %collective-permute-start.3 = (f32[1024,128]{1,0:T(8,128)}, f32[1024,128]{1,0:T(8,128)S(1)}, u32[]{:S(2)}, u32[]{:S(2)}) collective-permute-start(f32[1024,128]{1,0:T(8,128)} %all-reduce.7.cloned.1.call-done), channel_id=1, source_target_pairs={{0,4},{4,0},{8,12},{12,8},{16,20},{20,16},{24,28},{28,24},{32,36},... | collective-permute-start | bytes 1572872 | tf_op jit(solution)/shard_map/ppermute | solution.py:16
  281.0 1.0 copy-start.7
  291.8 49.0 %collective-permute-start.4 = (f32[1024,512]{1,0:T(8,128)}, f32[1024,512]{1,0:T(8,128)}, u32[]{:S(2)}, u32[]{:S(2)}) collective-permute-start(f32[1024,512]{1,0:T(8,128)} %convolution_subtract_fusion), channel_id=1, source_target_pairs={{0,8},{4,12},{8,0},{12,4},{16,24},{20,28},{24,16},{28,20},{32,40},... | collective-permute-start | bytes 6291464 | tf_op jit(solution)/shard_map/ppermute | solution.py:16
  349.2 1.7 copy-start.3
  361.1 144.1 %all-reduce.11.cloned.1.call-start = ((), (), s32[]{:S(2)}) async-start(), calls=%async_computation.5 | async-start | bytes 524288 | tf_op jit(solution)/shard_map/psum | solution.py:21
  417.7 6.1 %collective-permute-start.5 = (f32[512,128]{1,0:T(8,128)}, f32[512,128]{1,0:T(8,128)S(1)}, u32[]{:S(2)}, u32[]{:S(2)}) collective-permute-start(f32[512,128]{1,0:T(8,128)} %all-reduce.9.cloned.1.call-done), channel_id=1, source_target_pairs={{0,4},{4,0},{8,12},{12,8},{16,20},{20,16},{24,28},{28,24},{32,36},... | collective-permute-start | bytes 786440 | tf_op jit(solution)/shard_map/ppermute | solution.py:16
  425.6 15.2 %collective-permute-start.6 = (f32[2,512,128]{2,1,0:T(8,128)}, f32[2,512,128]{2,1,0:T(8,128)S(1)}, u32[]{:S(2)}, u32[]{:S(2)}) collective-permute-start(f32[2,512,128]{2,1,0:T(8,128)} %maximum_select_fusion.4), channel_id=1, source_target_pairs={{0,8},{4,12},{8,0},{12,4},{16,24},{20,28},{24,16},{28,20},{32,40},... | collective-permute-start | bytes 1572872 | tf_op jit(solution)/shard_map/ppermute | solution.py:16
  440.9 4.9 copy-start.5
  441.0 1.0 copy-start.8
  505.2 12.1 %copy-start.4 = (f32[512,128]{1,0:T(8,128)S(1)}, f32[512,128]{1,0:T(8,128)}, u32[]{:S(2)}) copy-start(f32[512,128]{1,0:T(8,128)} %all-reduce.11.cloned.1.call-done) | copy-start | bytes 786436
  505.2 6.2 %collective-permute-start.7 = (f32[512,128]{1,0:T(8,128)}, f32[512,128]{1,0:T(8,128)S(1)}, u32[]{:S(2)}, u32[]{:S(2)}) collective-permute-start(f32[512,128]{1,0:T(8,128)} %all-reduce.11.cloned.1.call-done), channel_id=1, source_target_pairs={{0,4},{4,0},{8,12},{12,8},{16,20},{20,16},{24,28},{28,24},{32,36},... | collective-permute-start | bytes 786440 | tf_op jit(solution)/shard_map/ppermute | solution.py:16
  513.3 15.3 %collective-permute-start.8 = (f32[2,512,128]{2,1,0:T(8,128)}, f32[2,512,128]{2,1,0:T(8,128)}, u32[]{:S(2)}, u32[]{:S(2)}) collective-permute-start(f32[2,512,128]{2,1,0:T(8,128)} %maximum_select_fusion.6), channel_id=1, source_target_pairs={{0,8},{4,12},{8,0},{12,4},{16,24},{20,28},{24,16},{28,20},{32,40},... | collective-permute-start | bytes 1572872 | tf_op jit(solution)/shard_map/ppermute | solution.py:16
  530.0 4.6 copy-start.1
Sparse Core Ops, SparseCore 0:
  154.6 46.6 all-reduce.4
  216.6 56.6 all-reduce.6
  361.2 56.4 all-reduce.8
  449.1 55.9 all-reduce.10
where the time goes:
time: 551 us; the launch traced here: 541 us
  waiting for transfers between devices  290 us (53%)
  other arithmetic  69.1 us (13%)
  starting transfers between devices  68.4 us (12%)
  local copies, waits for them, and re-layouts  55.6 us (10%)
  matrix products  23.5 us (4%)
  blocking collectives  19.6 us (4%)
  between operations  15 us (3%)
    psum x4, waiting for transfers between devices, from_root(): return lax.psum(jnp.where(mine, array, jnp.zeros_like(array)), axis)  216 us
    ppermute x9, waiting for transfers between devices, partner(): lax.ppermute(array, axis, [(i, i ^ 1 << stride) for i in range(lax.axis_s...  50.3 us
    ppermute x9, starting transfers between devices, partner(): lax.ppermute(array, axis, [(i, i ^ 1 << stride) for i in range(lax.axis_s...  40.1 us
    all_to_all x1, waiting for transfers between devices, local(): lax.all_to_all(send_values.reshape(cube_count, capacity, block_width), 'c...  19.3 us
    all_to_all x1, starting transfers between devices, local(): lax.all_to_all(send_rows.reshape(cube_count, capacity), 'cube', split_axi...  16.5 us
    scatter-add x1, other arithmetic, local(): jax.ops.segment_sum(jnp.swapaxes(child_terms, 1, 2).reshape(-1, child_row...  15 us
    scatter-add x1, other arithmetic, local(): jax.ops.segment_sum(by_cols, row_ids.reshape(-1), num_segments=half_rows...  13.8 us
    dot_general x4, matrix products, apply_panel(): jnp.dot(lower_rows, (col_rows * keep_cols).T, precision=HIGHEST)  12.1 us
  transfers between devices with their start and end apart: 15, of which 14 were waited for; matrix products, arithmetic and copies ran while one was open for 9% of the time, Pallas kernels for 0%

commit v1 on v0

v1 whole, which is shorter than its diff:
```python
import functools

import jax
import jax.numpy as jnp
from jax import lax
from jax.experimental import pallas as pl
from jax.experimental.pallas import tpu as pltpu
from jax.sharding import PartitionSpec as P

PIV = 128
QUARTER = 512
PLANE = 8
SLOTS = 40
CHUNKS = 12
F32 = jnp.float32
BF16 = jnp.bfloat16
MESH = pl.DeviceIdType.MESH
NN = (((1,), (0,)), ((), ()))
NT = (((1,), (1,)), ((), ()))


def mm(a, b, dims=NN):
    return lax.dot_general(a, b, dims, preferred_element_type=F32)


def exact(a, b, dims=NN):
    return lax.dot_general(
        a, b, dims, precision=lax.Precision.HIGHEST, preferred_element_type=F32
    )


def halves(a):
    high = a.astype(BF16)
    return high, (a - high.astype(F32)).astype(BF16)


def dot3(a, b, dims=NN):
    a_high, a_low = halves(a)
    b_high, b_low = halves(b)
    return mm(a_high, b_high, dims) + (mm(a_high, b_low, dims) + mm(a_low, b_high, dims))


def iota(shape, axis):
    return lax.broadcasted_iota(jnp.int32, shape, axis)


def hits(a, b):
    return jnp.where(a == b, 1.0, 0.0).astype(BF16)


def newton_inverse(block):
    eye = iota((PIV, PIV), 0) == iota((PIV, PIV), 1)
    on_diagonal = jnp.where(eye, block, 0.0)
    by_col = 1.0 / jnp.sum(on_diagonal, axis=0, keepdims=True)
    by_row = 1.0 / jnp.sum(on_diagonal, axis=1, keepdims=True)
    current = jnp.where(eye, 2.0 * by_col, 0.0) - by_row * (block * by_col)
    return 2.0 * current - exact(current, exact(block, current))


def fused(
    depth_z,
    blocks,
    owner,
    target,
    leaf_pivot,
    signs,
    perturb,
    leaf_coupling,
    leaf_map,
    mid,
    level,
    top,
    factor_out,
    mid_factor_out,
    upper_out,
    s1,
    r1,
    s2,
    r2,
    rbuf,
    piv,
    inv_sets,
    leaf_inv,
    lfull,
    l_high,
    l_low,
    p_high,
    p_low,
    vout,
    vin,
    kb,
    rt,
    kr_high,
    kr_low,
    zs,
    zr,
    ds,
    dr,
    ps,
    pr,
    es,
    er,
    vs,
    vr,
    ks,
    kr,
):
    cube = lax.axis_index("cube")
    front = lax.axis_index("front")
    pos_z = cube // PLANE
    pos_d = cube % PLANE
    low = cube % 2
    high = (cube // 2) % 2
    rho = 2 * low + high
    core_peer = cube + 1 - 2 * low
    y_peer = cube + 2 - 4 * high
    both_peer = core_peer + 2 - 4 * high
    plane_base = cube - pos_d
    group = cube // 2
    row_count = blocks.shape[1]
    cube_count = depth_z * PLANE

    def at_z(step):
        return (pos_z + step) % depth_z

    def at_plane(step):
        return (pos_d + step) % PLANE

    barrier = pltpu.get_barrier_semaphore()

    def greet_z(step, carry):
        pl.semaphore_signal(
            barrier, inc=1, device_id=(at_z(step) * PLANE + pos_d, front), device_id_type=MESH
        )
        return carry

    def greet_plane(step, carry):
        pl.semaphore_signal(
            barrier, inc=1, device_id=(plane_base + at_plane(step), front), device_id_type=MESH
        )
        return carry

    lax.fori_loop(1, depth_z, greet_z, 0)
    lax.fori_loop(1, PLANE, greet_plane, 0)
    for step in range(1, 4):
        pl.semaphore_signal(
            barrier, inc=1, device_id=(cube, (front + step) % 4), device_id_type=MESH
        )

    @pl.when(front == 0)
    def _():
        rbuf[0:1024, :] = mid[:, 0:256].astype(F32)
        rbuf[1536:2048, :] = top[:, 0:256].astype(F32)

    own = owner[...]
    own_mask = iota((cube_count, row_count), 0) == own
    own_hits = jnp.where(own_mask, 1.0, 0.0).astype(BF16)
    before = jnp.where(
        iota((row_count, row_count), 0) < iota((row_count, row_count), 1), 1.0, 0.0
    ).astype(BF16)
    ahead = mm(own_hits, before)
    rank = jnp.sum(jnp.where(own_mask, ahead, 0.0), axis=0, keepdims=True).astype(jnp.int32)
    base = (own >> 3) * SLOTS + (own & 7)
    send_rows = depth_z * SLOTS
    row_ids = iota((send_rows, row_count), 0)
    to_slot = hits(row_ids, base + rank * PLANE)
    value_high, value_low = halves(blocks[0])
    marks = jnp.where(row_ids == base + 32, (target[...] + 1).astype(F32), 0.0).astype(BF16)
    by_rank = hits(iota((PIV, row_count), 0), rank)
    s1[...] = mm(to_slot, value_high) + mm(to_slot, value_low) + mm(marks, by_rank, NT)

    pl.semaphore_wait(barrier, depth_z + PLANE + 1)

    def z_copy(step):
        there = at_z(step)
        return pltpu.make_async_remote_copy(
            src_ref=s1.at[pl.ds(pl.multiple_of(there * SLOTS, 8), SLOTS)],
            dst_ref=r1.at[pl.ds(pl.multiple_of(pos_z * SLOTS, 8), SLOTS)],
            send_sem=zs.at[step],
            recv_sem=zr.at[step],
            device_id=(there * PLANE + pos_d, front),
            device_id_type=MESH,
        )

    def start_z(step, carry):
        z_copy(step).start()
        return carry

    lax.fori_loop(1, depth_z, start_z, 0)

    def chunk_copy(index, there):
        rows = pl.ds(pl.multiple_of(index * PIV + 512 * (index // 8), PIV), PIV)
        return pltpu.make_async_remote_copy(
            src_ref=rbuf.at[rows],
            dst_ref=rbuf.at[rows],
            send_sem=ps.at[index],
            recv_sem=pr.at[index],
            device_id=(cube, there),
            device_id_type=MESH,
        )

    up = (front + 1) % 4
    down = (front + 3) % 4

    @pl.when(front == 0)
    def _():
        def push(index, carry):
            chunk_copy(index, up).start()
            chunk_copy(index + 6, down).start()
            return carry

        lax.fori_loop(0, 6, push, 0)

    own_rows = pl.ds(pl.multiple_of(pos_z * SLOTS, 8), SLOTS)
    r1[own_rows, :] = s1[own_rows, :]

    eye = iota((PIV, PIV), 0) == iota((PIV, PIV), 1)
    links = level[pl.ds(group, 1), :]
    two_rows = iota((16, 2048), 0)
    digits = jnp.where(two_rows == 0, links >> 4, jnp.where(two_rows == 1, links & 15, 0))
    digits = digits.astype(F32).astype(BF16)

    def prepare_leaf(leaf, carry):
        shift = signs[pl.ds(leaf, 1), :].astype(F32) * perturb[pl.ds(leaf, 1), :]
        leaf_inv[leaf] = newton_inverse(leaf_pivot[leaf] + jnp.where(eye, shift, 0.0))
        picked = mm(digits, hits(iota((2048, PIV), 0), leaf_map[pl.ds(leaf, 1), :]))
        composite = picked[0:1, :] * 16.0 + picked[1:2, :]
        kb[0, front, leaf, 128:136, :] = jnp.broadcast_to(composite, (8, PIV))
        return carry

    lax.fori_loop(0, 2, prepare_leaf, 0)

    @pl.when(front != 0)
    def _():
        def forward(index, carry):
            chunk_copy(index, up).wait_recv()

            @pl.when(front != 3)
            def _():
                chunk_copy(index, up).start()

            chunk_copy(index + 6, down).wait_recv()

            @pl.when(front != 1)
            def _():
                chunk_copy(index + 6, down).start()

            return carry

        lax.fori_loop(0, 6, forward, 0)

    col_g = pl.ds(1024, 512)
    col_u = pl.ds(2048, 512)
    holds_g = low == front // 2
    holds_u = rho == front
    first_g = pl.ds(pl.multiple_of((front % 2) * 512, 512), 512)
    pivot_g = pl.ds(0, 256)
    pivot_u = pl.ds(1536, 256)
    whole_u = pl.ds(1536, 512)
    peers = (core_peer, y_peer, both_peer)

    def edge(source, place, number, arrival, there):
        return pltpu.make_async_remote_copy(
            src_ref=source,
            dst_ref=place,
            send_sem=es.at[number],
            recv_sem=er.at[arrival],
            device_id=(there, front),
            device_id_type=MESH,
        )

    def edges_g():
        return edge(rbuf.at[first_g], rbuf.at[col_g], 0, 0, core_peer)

    def edges_pg():
        return edge(rbuf.at[pivot_g], piv.at[0], 1, 1, core_peer)

    def edges_u(which):
        return edge(rbuf.at[whole_u], rbuf.at[col_u], 2 + which, 2, peers[which])

    def edges_pu(which):
        return edge(rbuf.at[pivot_u], piv.at[1], 5 + which, 3, peers[which])

    @pl.when(low == 0)
    def _():
        edges_pg().start()
        piv[0] = rbuf[pivot_g, :]

    @pl.when(rho == 0)
    def _():
        for which in range(3):
            edges_pu(which).start()
        piv[1] = rbuf[pivot_u, :]

    @pl.when(holds_g)
    def _():
        edges_g().start()
        rbuf[col_g, :] = rbuf[first_g, :]

    @pl.when(holds_u)
    def _():
        for which in range(3):
            edges_u(which).start()
        rbuf[col_u, :] = rbuf[whole_u, :]

    def wait_z(step, carry):
        z_copy(step).wait_recv()
        return carry

    lax.fori_loop(1, depth_z, wait_z, 0)
    for place in range(PLANE):
        for slot in range(5):
            s2[place, slot] = r1[pl.ds(slot * PLANE + place, depth_z, stride=SLOTS), :]

    def d_copy(step):
        there = at_plane(step)
        return pltpu.make_async_remote_copy(
            src_ref=s2.at[there],
            dst_ref=r2.at[pos_d],
            send_sem=ds.at[step],
            recv_sem=dr.at[step],
            device_id=(plane_base + there, front),
            device_id_type=MESH,
        )

    def start_d(step, carry):
        d_copy(step).start()
        return carry

    lax.fori_loop(1, PLANE, start_d, 0)
    r2[pos_d] = s2[pos_d]

    @pl.when(low != 0)
    def _():
        edges_pg().wait_recv()

    @pl.when(rho != 0)
    def _():
        edges_pu(0).wait_recv()

    def invert_set(number, carry):
        rows_two = piv[number, 128:256, 0:128]
        first = newton_inverse(piv[number, 0:128, 0:128])
        second = newton_inverse(
            piv[number, 128:256, 128:256] - exact(exact(rows_two, first), rows_two, NT)
        )
        inv_sets[number, 0] = first
        inv_sets[number, 1] = second
        inv_sets[number, 2] = rows_two
        return carry

    lax.fori_loop(0, 2, invert_set, 0)

    def wait_d(step, carry):
        d_copy(step).wait_recv()
        return carry

    lax.fori_loop(1, PLANE, wait_d, 0)

    slots_per = PLANE * depth_z
    marks_in = r2[:, 4].reshape(slots_per, PIV).T.astype(jnp.int32)
    arrivals = jnp.zeros((256, PIV), F32)
    for slot in range(4):
        to_row = hits(iota((256, slots_per), 0) + 1, marks_in[slot : slot + 1, :])
        got_high, got_low = halves(r2[:, slot].reshape(slots_per, PIV))
        arrivals = arrivals + mm(to_row, got_high) + mm(to_row, got_low)
    for leaf in range(2):
        coupling = leaf_coupling[leaf] + arrivals[leaf * PIV : (leaf + 1) * PIV, :]
        factor = exact(coupling, leaf_inv[leaf])
        factor_out[leaf] = factor
        kb[0, front, leaf, 0:128, :] = -exact(factor, coupling, NT)

    def k_copy(source, place, where, send, arrival, there):
        return pltpu.make_async_remote_copy(
            src_ref=kb.at[source, where],
            dst_ref=kb.at[place, where],
            send_sem=ks.at[send],
            recv_sem=kr.at[arrival],
            device_id=there,
            device_id_type=MESH,
        )

    def k_y():
        return k_copy(0, 2, front, 0, 0, (y_peer, front))

    def k_front(which, step):
        number = 1 + 3 * which + step - 1
        return k_copy(
            2 * which, 2 * which, front, number, number, (cube, (front + step) % 4)
        )

    def k_core(which, step):
        number = 7 + 4 * which + step
        return k_copy(
            2 * which,
            2 * which + 1,
            (front + 4 - step) % 4,
            number,
            number,
            (core_peer, front),
        )

    k_y().start()
    for step in (1, 3, 2):
        k_front(0, step).start()
    k_core(0, 0).start()

    @pl.when(low != front // 2)
    def _():
        edges_g().wait_recv()

    def panel(index, carry):
        number = index // 3
        start = jnp.where(
            index < 2,
            low * 1024 + index * 512,
            jnp.where(index == 3, rho * 512, front * 512),
        )
        rows = pl.ds(pl.multiple_of(index * 512, 512), 512)
        place = iota((512, PIV), 0) + start
        first = rbuf[rows, 0:128]
        second = rbuf[rows, 128:256]
        past_one = place >= 128
        past_two = place >= 256
        lower_one = jnp.where(past_one, dot3(first, inv_sets[number, 0]), 0.0)
        second = second - dot3(lower_one, inv_sets[number, 2], NT)
        lower_two = jnp.where(past_two, dot3(second, inv_sets[number, 1]), 0.0)
        lfull[rows, 0:128] = lower_one
        lfull[rows, 128:256] = lower_two
        one_high, one_low = halves(lower_one)
        two_high, two_low = halves(lower_two)
        l_high[rows, 0:128] = one_high
        l_high[rows, 128:256] = two_high
        l_low[rows, 0:128] = one_low
        l_low[rows, 128:256] = two_low
        one_high, one_low = halves(jnp.where(past_one, first, 0.0))
        two_high, two_low = halves(jnp.where(past_two, second, 0.0))
        p_high[rows, 0:128] = one_high
        p_high[rows, 128:256] = two_high
        p_low[rows, 0:128] = one_low
        p_low[rows, 128:256] = two_low
        return carry

    lax.fori_loop(0, 3, panel, 0)

    def update(l_rows, p_rows):
        return mm(l_high[l_rows, :], p_high[p_rows, :], NT) + (
            mm(l_high[l_rows, :], p_low[p_rows, :], NT)
            + mm(l_low[l_rows, :], p_high[p_rows, :], NT)
        )

    def quarter_map(quarter):
        entries = level[pl.ds(group, 1), pl.ds(pl.multiple_of(quarter * 512, 512), 512)]
        kept = iota((1, 512), 1) + quarter * 512 >= 256
        return hits(iota((512, 512), 0), jnp.where(kept, entries - quarter * 512, -1))

    col_hits = quarter_map(front)

    def link(turn, carry):
        half = turn * high + (1 - turn) * (1 - high)
        rows = pl.ds(pl.multiple_of(half * 512, 512), 512)
        schur = mid[rows, :].astype(F32) - update(rows, col_g)
        s_high, s_low = halves(schur)
        t_high, t_low = halves(mm(s_high, col_hits, NT) + mm(s_low, col_hits, NT))
        row_hits = quarter_map(2 * low + half)
        vout[turn] = mm(row_hits, t_high) + mm(row_hits, t_low)
        return carry

    def v_copy():
        return pltpu.make_async_remote_copy(
            src_ref=vout.at[0],
            dst_ref=vin,
            send_sem=vs.at[0],
            recv_sem=vr.at[0],
            device_id=(y_peer, front),
            device_id_type=MESH,
        )

    k_y().wait_recv()
    for step in (1, 3, 2):
        k_front(1, step).start()
    k_core(1, 0).start()
    lax.fori_loop(0, 1, link, 0)
    v_copy().start()
    lax.fori_loop(1, 2, link, 0)

    @pl.when(rho != front)
    def _():
        edges_u(0).wait_recv()

    lax.fori_loop(3, 5, panel, 0)
    mid_factor_out[...] = lfull[pl.ds(pl.multiple_of(front * 256, 256), 256), :]
    upper_out[...] = top[...].astype(F32) - update(whole_u, col_u) + vout[1]

    ids = iota((512, PIV), 0)

    def gather_group(which, carry):
        def one(index, inner):
            entry = index // 2
            leaf = index % 2
            composite = kb[which, entry, leaf, 128:129, :].astype(jnp.int32)
            cols = pl.ds(pl.multiple_of(index * PIV, PIV), PIV)
            rt[:, cols] = hits(ids, composite - rho * 512)
            col_ids = hits(ids, composite - front * 512)
            k_high, k_low = halves(kb[which, entry, leaf, 0:128, :])
            spread_high, spread_low = halves(mm(k_high, col_ids, NT) + mm(k_low, col_ids, NT))
            kr_high[cols, :] = spread_high
            kr_low[cols, :] = spread_low
            return inner

        lax.fori_loop(0, 8, one, 0)
        upper_out[...] += mm(rt[...], kr_high[...]) + mm(rt[...], kr_low[...])
        return carry

    for step in (1, 3, 2):
        k_front(0, step).wait_recv()
        k_core(0, step).start()
        k_front(1, step).wait_recv()
        k_core(1, step).start()
    lax.fori_loop(0, 2, lambda turn, carry: gather_group(2 * turn, carry), 0)
    v_copy().wait_recv()
    upper_out[...] += vin[...]
    for step in range(4):
        k_core(0, step).wait_recv()
        k_core(1, step).wait_recv()
    lax.fori_loop(0, 2, lambda turn, carry: gather_group(2 * turn + 1, carry), 0)

    def end_z(step, carry):
        z_copy(step).wait_send()
        return carry

    def end_d(step, carry):
        d_copy(step).wait_send()
        return carry

    lax.fori_loop(1, depth_z, end_z, 0)
    lax.fori_loop(1, PLANE, end_d, 0)

    @pl.when(front != 3)
    def _():
        def end_up(index, carry):
            chunk_copy(index, up).wait_send()
            return carry

        lax.fori_loop(0, 6, end_up, 0)

    @pl.when(front != 1)
    def _():
        def end_down(index, carry):
            chunk_copy(index, down).wait_send()
            return carry

        lax.fori_loop(6, 12, end_down, 0)

    @pl.when(low == 0)
    def _():
        edges_pg().wait_send()

    @pl.when(holds_g)
    def _():
        edges_g().wait_send()

    @pl.when(rho == 0)
    def _():
        for which in range(3):
            edges_pu(which).wait_send()

    @pl.when(holds_u)
    def _():
        for which in range(3):
            edges_u(which).wait_send()

    v_copy().wait_send()
    k_y().wait_send()
    for which in range(2):
        for step in range(1, 4):
            k_front(which, step).wait_send()
        for step in range(4):
            k_core(which, step).wait_send()


def local(
    kkt_blocks,
    kkt_owner,
    kkt_target,
    leaf_pivot,
    pivot_signs,
    perturb,
    leaf_coupling,
    leaf_map,
    mid_front,
    level_map,
    top_front,
):
    depth_z = lax.axis_size("cube") // PLANE
    vmem = pl.BlockSpec(memory_space=pltpu.VMEM)
    dma = pltpu.SemaphoreType.DMA
    return pl.pallas_call(
        functools.partial(fused, depth_z),
        out_shape=(
            jax.ShapeDtypeStruct((2, PIV, PIV), F32),
            jax.ShapeDtypeStruct((256, 256), F32),
            jax.ShapeDtypeStruct((512, 512), F32),
        ),
        in_specs=[vmem] * 11,
        out_specs=(vmem, vmem, vmem),
        scratch_shapes=[
            pltpu.VMEM((depth_z * SLOTS, PIV), F32),
            pltpu.VMEM((depth_z * SLOTS, PIV), F32),
            pltpu.VMEM((PLANE, 5, depth_z, PIV), F32),
            pltpu.VMEM((PLANE, 5, depth_z, PIV), F32),
            pltpu.VMEM((2560, 256), F32),
            pltpu.VMEM((2, 256, 256), F32),
            pltpu.VMEM((2, 3, PIV, PIV), F32),
            pltpu.VMEM((2, PIV, PIV), F32),
            pltpu.VMEM((2560, 256), F32),
            pltpu.VMEM((2560, 256), BF16),
            pltpu.VMEM((2560, 256), BF16),
            pltpu.VMEM((2560, 256), BF16),
            pltpu.VMEM((2560, 256), BF16),
            pltpu.VMEM((2, 512, 512), F32),
            pltpu.VMEM((512, 512), F32),
            pltpu.VMEM((4, 4, 2, 136, PIV), F32),
            pltpu.VMEM((512, 1024), BF16),
            pltpu.VMEM((1024, 512), BF16),
            pltpu.VMEM((1024, 512), BF16),
            dma((depth_z,)),
            dma((depth_z,)),
            dma((PLANE,)),
            dma((PLANE,)),
            dma((CHUNKS,)),
            dma((CHUNKS,)),
            dma((8,)),
            dma((4,)),
            dma((1,)),
            dma((1,)),
            dma((15,)),
            dma((15,)),
        ],
        compiler_params=pltpu.CompilerParams(
            collective_id=0, has_side_effects=True, vmem_limit_bytes=56 * 1024 * 1024
        ),
    )(
        kkt_blocks,
        kkt_owner.reshape(1, -1),
        kkt_target,
        leaf_pivot,
        pivot_signs,
        perturb,
        leaf_coupling,
        leaf_map,
        mid_front,
        level_map,
        top_front,
    )


def solution(mesh):
    in_specs = (
        P("front", "cube", None),
        P("front", "cube", None),
        P("front", "cube"),
        P("cube", "front", None),
        P("cube", "front"),
        P("cube", "front"),
        P("cube", "front", None),
        P("cube", "front"),
        P("cube", "front"),
        P(),
        P("cube", "front"),
    )
    out_specs = (P("cube", "front", None), P(("cube", "front"), None), P("cube", "front"))
    return jax.shard_map(local, mesh=mesh, in_specs=in_specs, out_specs=out_specs, check_vma=False)
```

time: 551 us -> 183 us (0.33)
  the two profiles are of different devices: /device:TPU:1 before, /device:TPU:2 now
where the time goes in v1:
time: 183 us
  Pallas kernels  178 us (97%)
  local copies, waits for them, and re-layouts  4.58 us (3%)
    pallas_call x1, Pallas kernels, local(): pl.pallas_call(functools.partial(fused, depth_z), out_shape=(jax.ShapeDty...  178 us
    unnamed x5, local copies, waits for them, and re-layouts  4.58 us

profile of v1, /device:TPU:2, one launch (start us, length us, event | category | flops | bytes accessed | tf_op | source)
XLA Modules:
  0.0 183.2 jit_solution(11081143346530368735)
XLA Ops:
  0.6 177.9 %shard_map.130 = (f32[2,128,128]{2,1,0:T(8,128)}, f32[256,256]{1,0:T(8,128)}, f32[512,512]{1,0:T(8,128)}) custom-call(f32[1,256,128]{2,1,0:T(8,128)} %blocks.1, s32[1,256]{1,0:T(1,128)} %bitcast.1, s32[1,256]{1,0:T(1,128)} %target.1, f32[2,128,128]{2,1,0:T(8,128)} %leaf_pivot.1, s32[2,128]{1,0:T(2,128)} %signs.1, f32[2,128]{1,0:T(2,128)} %perturb.1, ...), custom_call_target="tpu_custom_call" | custom-call | tf_op jit(solution)/shard_map/pallas_call | solution.py:598
  178.6 0.0 copy-start
  178.6 1.6 copy.17
  180.2 0.0 copy-done
  180.2 0.7 copy.18
  180.9 2.3 %copy.19 = f32[512,512]{1,0:T(8,128)} copy(f32[512,512]{1,0:T(8,128)} %get-tuple-element.8) | data formatting | bytes 2097152
Async XLA Ops:
  178.6 1.6 copy-start

commit v2 on v1

--- a/solution.py
+++ b/solution.py
@@ -11,7 +11,8 @@
 QUARTER = 512
 PLANE = 8
 SLOTS = 40
-CHUNKS = 12
+CHUNK = 32
+HALF = 16
 F32 = jnp.float32
 BF16 = jnp.bfloat16
 MESH = pl.DeviceIdType.MESH
@@ -78,6 +79,7 @@
     s2,
     r2,
     rbuf,
+    relay,
     piv,
     inv_sets,
     leaf_inv,
@@ -98,8 +100,16 @@
     dr,
     ps,
     pr,
+    gs,
+    gr,
+    hs,
+    hr,
+    us,
+    ur,
     es,
     er,
+    xs,
+    xr,
     vs,
     vr,
     ks,
@@ -114,7 +124,6 @@
     rho = 2 * low + high
     core_peer = cube + 1 - 2 * low
     y_peer = cube + 2 - 4 * high
-    both_peer = core_peer + 2 - 4 * high
     plane_base = cube - pos_d
     group = cube // 2
     row_count = blocks.shape[1]
@@ -189,7 +198,7 @@
     lax.fori_loop(1, depth_z, start_z, 0)
 
     def chunk_copy(index, there):
-        rows = pl.ds(pl.multiple_of(index * PIV + 512 * (index // 8), PIV), PIV)
+        rows = pl.ds(pl.multiple_of(index * CHUNK, CHUNK), CHUNK)
         return pltpu.make_async_remote_copy(
             src_ref=rbuf.at[rows],
             dst_ref=rbuf.at[rows],
@@ -201,15 +210,141 @@
 
     up = (front + 1) % 4
     down = (front + 3) % 4
+    holds_g = low == front // 2
+    holds_u = rho == front
+    col_g = pl.ds(1024, 512)
+    col_u = pl.ds(2048, 512)
+    first_g = pl.ds(pl.multiple_of((front % 2) * 512, 512), 512)
+    pivot_g = pl.ds(0, 256)
+    pivot_u = pl.ds(1536, 256)
+    whole_u = pl.ds(1536, 512)
+
+    def col_copy(part):
+        start = (front % 2) * 512 + part * CHUNK
+        return pltpu.make_async_remote_copy(
+            src_ref=rbuf.at[pl.ds(pl.multiple_of(start, CHUNK), CHUNK)],
+            dst_ref=rbuf.at[pl.ds(pl.multiple_of(1024 + part * CHUNK, CHUNK), CHUNK)],
+            send_sem=gs.at[part],
+            recv_sem=gr.at[part],
+            device_id=(core_peer, front),
+            device_id_type=MESH,
+        )
+
+    def pivot_copy(part):
+        rows = pl.ds(pl.multiple_of(part * CHUNK, CHUNK), CHUNK)
+        return pltpu.make_async_remote_copy(
+            src_ref=rbuf.at[rows],
+            dst_ref=piv.at[0, rows],
+            send_sem=hs.at[part],
+            recv_sem=hr.at[part],
+            device_id=(core_peer, front),
+            device_id_type=MESH,
+        )
+
+    def landed(index):
+        @pl.when((low == 0) & (index < 8))
+        def _():
+            pivot_copy(index).start()
+
+        @pl.when(holds_g & (index // HALF == front % 2))
+        def _():
+            col_copy(index % HALF).start()
+
+    def upper_copy(half, there, number):
+        rows = pl.ds(pl.multiple_of(1536 + 256 * half, 256), 256)
+        return pltpu.make_async_remote_copy(
+            src_ref=rbuf.at[rows],
+            dst_ref=rbuf.at[rows],
+            send_sem=us.at[number],
+            recv_sem=ur.at[half],
+            device_id=(cube, there),
+            device_id_type=MESH,
+        )
+
+    def edge(source, place, number, arrival, there):
+        return pltpu.make_async_remote_copy(
+            src_ref=source,
+            dst_ref=place,
+            send_sem=es.at[number],
+            recv_sem=er.at[arrival],
+            device_id=(there, front),
+            device_id_type=MESH,
+        )
+
+    def edge_col(number, there):
+        return edge(rbuf.at[whole_u], rbuf.at[col_u], number, 0, there)
+
+    def edge_col_on():
+        return edge(rbuf.at[col_u], rbuf.at[col_u], 0, 0, core_peer)
+
+    def edge_pivot(number, there):
+        return edge(rbuf.at[pivot_u], piv.at[1], 2 + number, 1, there)
+
+    def edge_pivot_on():
+        return edge(piv.at[1], piv.at[1], 2, 1, core_peer)
+
+    def relay_copy():
+        return pltpu.make_async_remote_copy(
+            src_ref=rbuf.at[whole_u],
+            dst_ref=relay,
+            send_sem=xs.at[0],
+            recv_sem=xr.at[0],
+            device_id=(y_peer, front),
+            device_id_type=MESH,
+        )
+
+    def relay_on():
+        return pltpu.make_async_remote_copy(
+            src_ref=relay,
+            dst_ref=rbuf.at[col_u],
+            send_sem=xs.at[0],
+            recv_sem=er.at[0],
+            device_id=(cube, 2),
+            device_id_type=MESH,
+        )
+
+    relays = (front == 0) & (rho == 2)
+    relays_on = (front == 0) & (rho == 3)
+
+    def start_edges():
+        @pl.when(rho == 0)
+        def _():
+            edge_pivot(0, core_peer).start()
+            edge_pivot(1, y_peer).start()
+            piv[1] = rbuf[pivot_u, :]
+
+        @pl.when(holds_u)
+        def _():
+            edge_col(0, core_peer).start()
+
+            @pl.when(front != 2)
+            def _():
+                edge_col(1, y_peer).start()
+
+            rbuf[col_u, :] = rbuf[whole_u, :]
 
     @pl.when(front == 0)
     def _():
         def push(index, carry):
             chunk_copy(index, up).start()
-            chunk_copy(index + 6, down).start()
+            chunk_copy(index + HALF, down).start()
             return carry
 
-        lax.fori_loop(0, 6, push, 0)
+        lax.fori_loop(0, HALF, push, 0)
+
+        def push_core(index, carry):
+            landed(index)
+            return carry
+
+        lax.fori_loop(0, 2 * HALF, push_core, 0)
+        for half in range(2):
+            upper_copy(half, 1, 2 * half).start()
+            upper_copy(half, 3, 2 * half + 1).start()
+        start_edges()
+
+    @pl.when(relays)
+    def _():
+        relay_copy().start()
 
     own_rows = pl.ds(pl.multiple_of(pos_z * SLOTS, 8), SLOTS)
     r1[own_rows, :] = s1[own_rows, :]
@@ -230,78 +365,32 @@
 
     lax.fori_loop(0, 2, prepare_leaf, 0)
 
-    @pl.when(front != 0)
+    @pl.when((front == 1) | (front == 2))
     def _():
         def forward(index, carry):
             chunk_copy(index, up).wait_recv()
-
-            @pl.when(front != 3)
+            chunk_copy(index, up).start()
+            landed(index)
+
+            @pl.when(front == 2)
             def _():
-                chunk_copy(index, up).start()
-
-            chunk_copy(index + 6, down).wait_recv()
-
-            @pl.when(front != 1)
-            def _():
-                chunk_copy(index + 6, down).start()
+                chunk_copy(index + HALF, down).wait_recv()
+                chunk_copy(index + HALF, down).start()
+                landed(index + HALF)
 
             return carry
 
-        lax.fori_loop(0, 6, forward, 0)
-
-    col_g = pl.ds(1024, 512)
-    col_u = pl.ds(2048, 512)
-    holds_g = low == front // 2
-    holds_u = rho == front
-    first_g = pl.ds(pl.multiple_of((front % 2) * 512, 512), 512)
-    pivot_g = pl.ds(0, 256)
-    pivot_u = pl.ds(1536, 256)
-    whole_u = pl.ds(1536, 512)
-    peers = (core_peer, y_peer, both_peer)
-
-    def edge(source, place, number, arrival, there):
-        return pltpu.make_async_remote_copy(
-            src_ref=source,
-            dst_ref=place,
-            send_sem=es.at[number],
-            recv_sem=er.at[arrival],
-            device_id=(there, front),
-            device_id_type=MESH,
-        )
-
-    def edges_g():
-        return edge(rbuf.at[first_g], rbuf.at[col_g], 0, 0, core_peer)
-
-    def edges_pg():
-        return edge(rbuf.at[pivot_g], piv.at[0], 1, 1, core_peer)
-
-    def edges_u(which):
-        return edge(rbuf.at[whole_u], rbuf.at[col_u], 2 + which, 2, peers[which])
-
-    def edges_pu(which):
-        return edge(rbuf.at[pivot_u], piv.at[1], 5 + which, 3, peers[which])
-
-    @pl.when(low == 0)
-    def _():
-        edges_pg().start()
-        piv[0] = rbuf[pivot_g, :]
-
-    @pl.when(rho == 0)
-    def _():
-        for which in range(3):
-            edges_pu(which).start()
-        piv[1] = rbuf[pivot_u, :]
-
-    @pl.when(holds_g)
-    def _():
-        edges_g().start()
-        rbuf[col_g, :] = rbuf[first_g, :]
-
-    @pl.when(holds_u)
-    def _():
-        for which in range(3):
-            edges_u(which).start()
-        rbuf[col_u, :] = rbuf[whole_u, :]
+        lax.fori_loop(0, HALF, forward, 0)
+
+    @pl.when(front == 3)
+    def _():
+        def forward(index, carry):
+            chunk_copy(index + HALF, down).wait_recv()
+            chunk_copy(index + HALF, down).start()
+            landed(index + HALF)
+            return carry
+
+        lax.fori_loop(0, HALF, forward, 0)
 
     def wait_z(step, carry):
         z_copy(step).wait_recv()
@@ -330,13 +419,20 @@
     lax.fori_loop(1, PLANE, start_d, 0)
     r2[pos_d] = s2[pos_d]
 
-    @pl.when(low != 0)
-    def _():
-        edges_pg().wait_recv()
-
-    @pl.when(rho != 0)
-    def _():
-        edges_pu(0).wait_recv()
+    @pl.when(relays_on)
+    def _():
+        relay_copy().wait_recv()
+        relay_on().start()
+
+    @pl.when((front == 1) | (front == 3))
+    def _():
+        def take(index, carry):
+            number = index + (HALF // 2) * (3 - front)
+            chunk_copy(number, up).wait_recv()
+            landed(number)
+            return carry
+
+        lax.fori_loop(0, HALF, take, 0)
 
     def invert_set(number, carry):
         rows_two = piv[number, 128:256, 0:128]
@@ -348,8 +444,6 @@
         inv_sets[number, 1] = second
         inv_sets[number, 2] = rows_two
         return carry
-
-    lax.fori_loop(0, 2, invert_set, 0)
 
     def wait_d(step, carry):
         d_copy(step).wait_recv()
@@ -405,9 +499,20 @@
         k_front(0, step).start()
     k_core(0, 0).start()
 
-    @pl.when(low != front // 2)
-    def _():
-        edges_g().wait_recv()
+    @pl.when(low == 0)
+    def _():
+        piv[0] = rbuf[pivot_g, :]
+
+    @pl.when(low != 0)
+    def _():
+        for part in range(8):
+            pivot_copy(part).wait_recv()
+
+    @pl.when(holds_g)
+    def _():
+        rbuf[col_g, :] = rbuf[first_g, :]
+
+    lax.fori_loop(0, 1, invert_set, 0)
 
     def panel(index, carry):
         number = index // 3
@@ -441,7 +546,14 @@
         p_low[rows, 128:256] = two_low
         return carry
 
-    lax.fori_loop(0, 3, panel, 0)
+    lax.fori_loop(0, 2, panel, 0)
+
+    @pl.when(low != front // 2)
+    def _():
+        for part in range(HALF):
+            col_copy(part).wait_recv()
+
+    lax.fori_loop(2, 3, panel, 0)
 
     def update(l_rows, p_rows):
         return mm(l_high[l_rows, :], p_high[p_rows, :], NT) + (
@@ -466,31 +578,57 @@
         vout[turn] = mm(row_hits, t_high) + mm(row_hits, t_low)
         return carry
 
-    def v_copy():
-        return pltpu.make_async_remote_copy(
-            src_ref=vout.at[0],
-            dst_ref=vin,
-            send_sem=vs.at[0],
-            recv_sem=vr.at[0],
+    def v_copy(half):
+        rows = pl.ds(256 * half, 256)
+        return pltpu.make_async_remote_copy(
+            src_ref=vout.at[0, rows],
+            dst_ref=vin.at[rows],
+            send_sem=vs.at[half],
+            recv_sem=vr.at[half],
             device_id=(y_peer, front),
             device_id_type=MESH,
         )
+
+    lax.fori_loop(0, 1, link, 0)
+    @pl.when(rho != 1)
+    def _():
+        v_copy(0).start()
+
+    v_copy(1).start()
+    @pl.when((front == 1) | (front == 3))
+    def _():
+        half_one = pl.ds(pl.multiple_of(1536 + 128 * (front - 1), 256), 256)
+        passed = pltpu.make_async_remote_copy(
+            src_ref=rbuf.at[half_one],
+            dst_ref=rbuf.at[half_one],
+            send_sem=us.at[0],
+            recv_sem=ur.at[(front - 1) // 2],
+            device_id=(cube, 2),
+            device_id_type=MESH,
+        )
+        passed.wait_recv()
+        passed.start()
+
+    @pl.when((front == 1) | (front == 3))
+    def _():
+        upper_copy(1 - (front - 1) // 2, 1, 0).wait_recv()
+        start_edges()
+
+
+    mid_factor_out[...] = lfull[pl.ds(pl.multiple_of(front * 256, 256), 256), :]
 
     k_y().wait_recv()
     for step in (1, 3, 2):
         k_front(1, step).start()
     k_core(1, 0).start()
-    lax.fori_loop(0, 1, link, 0)
-    v_copy().start()
     lax.fori_loop(1, 2, link, 0)
-
-    @pl.when(rho != front)
-    def _():
-        edges_u(0).wait_recv()
-
-    lax.fori_loop(3, 5, panel, 0)
-    mid_factor_out[...] = lfull[pl.ds(pl.multiple_of(front * 256, 256), 256), :]
-    upper_out[...] = top[...].astype(F32) - update(whole_u, col_u) + vout[1]
+    upper_out[...] = top[...].astype(F32) + vout[1]
+
+    @pl.when(front == 2)
+    def _():
+        upper_copy(0, 1, 0).wait_recv()
+        upper_copy(1, 1, 0).wait_recv()
+        start_edges()
 
     ids = iota((512, PIV), 0)
 
@@ -508,7 +646,7 @@
             kr_low[cols, :] = spread_low
             return inner
 
-        lax.fori_loop(0, 8, one, 0)
+        lax.fori_loop(0, 8, one, 0, unroll=True)
         upper_out[...] += mm(rt[...], kr_high[...]) + mm(rt[...], kr_low[...])
         return carry
 
@@ -517,14 +655,47 @@
         k_core(0, step).start()
         k_front(1, step).wait_recv()
         k_core(1, step).start()
+
     lax.fori_loop(0, 2, lambda turn, carry: gather_group(2 * turn, carry), 0)
-    v_copy().wait_recv()
-    upper_out[...] += vin[...]
+
+    rho_y = rho + 1 - 2 * high
+
+    @pl.when(rho_y == 0)
+    def _():
+        edge_pivot(0, core_peer).wait_recv()
+        edge_pivot_on().start()
+
+    @pl.when(rho_y == front)
+    def _():
+        edge_col(0, core_peer).wait_recv()
+        edge_col_on().start()
+
     for step in range(4):
         k_core(0, step).wait_recv()
         k_core(1, step).wait_recv()
     lax.fori_loop(0, 2, lambda turn, carry: gather_group(2 * turn + 1, carry), 0)
 
+    @pl.when((rho != 0) & (rho_y != 0))
+    def _():
+        edge_pivot(0, core_peer).wait_recv()
+
+    lax.fori_loop(1, 2, invert_set, 0)
+    lax.fori_loop(3, 4, panel, 0)
+
+    @pl.when((rho != front) & (rho_y != front))
+    def _():
+        edge_col(0, core_peer).wait_recv()
+
+    lax.fori_loop(4, 5, panel, 0)
+    upper_out[...] += -update(whole_u, col_u)
+    v_copy(1).wait_recv()
+    upper_out[256:512, :] += vin[256:512, :]
+
+    @pl.when(rho != 0)
+    def _():
+        v_copy(0).wait_recv()
+        upper_out[0:256, :] += vin[0:256, :]
+
     def end_z(step, carry):
         z_copy(step).wait_send()
         return carry
@@ -542,7 +713,7 @@
             chunk_copy(index, up).wait_send()
             return carry
 
-        lax.fori_loop(0, 6, end_up, 0)
+        lax.fori_loop(0, HALF, end_up, 0)
 
     @pl.when(front != 1)
     def _():
@@ -550,33 +721,73 @@
             chunk_copy(index, down).wait_send()
             return carry
 
-        lax.fori_loop(6, 12, end_down, 0)
+        lax.fori_loop(HALF, 2 * HALF, end_down, 0)
 
     @pl.when(low == 0)
     def _():
-        edges_pg().wait_send()
+        for part in range(8):
+            pivot_copy(part).wait_send()
 
     @pl.when(holds_g)
     def _():
-        edges_g().wait_send()
+        for part in range(HALF):
+            col_copy(part).wait_send()
+
+    @pl.when(front == 0)
+    def _():
+        for number in range(4):
+            upper_copy(0, 1, number).wait_send()
+
+    @pl.when((front == 1) | (front == 3))
+    def _():
+        upper_copy(0, 2, 0).wait_send()
 
     @pl.when(rho == 0)
     def _():
-        for which in range(3):
-            edges_pu(which).wait_send()
+        edge_pivot(0, core_peer).wait_send()
+        edge_pivot(1, y_peer).wait_send()
+
+    @pl.when(rho_y == 0)
+    def _():
+        edge_pivot_on().wait_send()
 
     @pl.when(holds_u)
     def _():
-        for which in range(3):
-            edges_u(which).wait_send()
-
-    v_copy().wait_send()
+        edge_col(0, core_peer).wait_send()
+
+        @pl.when(front != 2)
+        def _():
+            edge_col(1, y_peer).wait_send()
+
+    @pl.when(relays)
+    def _():
+        relay_copy().wait_send()
+
+    @pl.when(relays_on)
+    def _():
+        relay_on().wait_send()
+
+    @pl.when(rho_y == front)
+    def _():
+        edge_col_on().wait_send()
+
+    v_copy(1).wait_send()
+
+    @pl.when(rho != 1)
+    def _():
+        v_copy(0).wait_send()
     k_y().wait_send()
     for which in range(2):
         for step in range(1, 4):
             k_front(which, step).wait_send()
         for step in range(4):
             k_core(which, step).wait_send()
+
+
+def hand_out(factor_in, mid_factor_in, upper_in, factor_out, mid_factor_out, upper_out):
+    factor_out[...] = factor_in[...]
+    mid_factor_out[...] = mid_factor_in[...]
+    upper_out[...] = upper_in[...]
 
 
 def local(
@@ -595,13 +806,14 @@
     depth_z = lax.axis_size("cube") // PLANE
     vmem = pl.BlockSpec(memory_space=pltpu.VMEM)
     dma = pltpu.SemaphoreType.DMA
-    return pl.pallas_call(
+    results = (
+        jax.ShapeDtypeStruct((2, PIV, PIV), F32),
+        jax.ShapeDtypeStruct((256, 256), F32),
+        jax.ShapeDtypeStruct((512, 512), F32),
+    )
+    computed = pl.pallas_call(
         functools.partial(fused, depth_z),
-        out_shape=(
-            jax.ShapeDtypeStruct((2, PIV, PIV), F32),
-            jax.ShapeDtypeStruct((256, 256), F32),
-            jax.ShapeDtypeStruct((512, 512), F32),
-        ),
+        out_shape=results,
         in_specs=[vmem] * 11,
         out_specs=(vmem, vmem, vmem),
         scratch_shapes=[
@@ -610,6 +822,7 @@
             pltpu.VMEM((PLANE, 5, depth_z, PIV), F32),
             pltpu.VMEM((PLANE, 5, depth_z, PIV), F32),
             pltpu.VMEM((2560, 256), F32),
+            pltpu.VMEM((512, 256), F32),
             pltpu.VMEM((2, 256, 256), F32),
             pltpu.VMEM((2, 3, PIV, PIV), F32),
             pltpu.VMEM((2, PIV, PIV), F32),
@@ -628,12 +841,20 @@
             dma((depth_z,)),
             dma((PLANE,)),
             dma((PLANE,)),
-            dma((CHUNKS,)),
-            dma((CHUNKS,)),
+            dma((2 * HALF,)),
+            dma((2 * HALF,)),
+            dma((HALF,)),
+            dma((HALF,)),
+            dma((8,)),
             dma((8,)),
             dma((4,)),
+            dma((2,)),
+            dma((4,)),
+            dma((2,)),
             dma((1,)),
             dma((1,)),
+            dma((2,)),
+            dma((2,)),
             dma((15,)),
             dma((15,)),
         ],
@@ -653,6 +874,12 @@
         level_map,
         top_front,
     )
+    return pl.pallas_call(
+        hand_out,
+        out_shape=results,
+        in_specs=[vmem] * 3,
+        out_specs=(vmem,) * 3,
+    )(*computed)
 
 
 def solution(mesh):

time: 183 us -> 87.7 us (0.48)
  the two profiles are of different devices: /device:TPU:2 before, /device:TPU:12 now
where the time goes in v2:
time: 87.7 us; the launch traced here: 87.5 us
  Pallas kernels  86.8 us (99%)
    pallas_call x1, Pallas kernels, local(): pl.pallas_call(functools.partial(fused, depth_z), out_shape=results, in_s...  84.4 us
    pallas_call x1, Pallas kernels, local(): pl.pallas_call(hand_out, out_shape=results, in_specs=[vmem] * 3, out_spec...  2.49 us

profile of v2, /device:TPU:12, one launch (start us, length us, event | category | flops | bytes accessed | tf_op | source)
XLA Modules:
  0.0 87.5 jit_solution(4476190241978641937)
XLA Ops:
  0.6 84.4 %shard_map.130 = (f32[2,128,128]{2,1,0:T(8,128)}, f32[256,256]{1,0:T(8,128)}, f32[512,512]{1,0:T(8,128)}) custom-call(f32[1,256,128]{2,1,0:T(8,128)} %blocks.1, s32[1,256]{1,0:T(1,128)} %bitcast.1, s32[1,256]{1,0:T(1,128)} %target.1, f32[2,128,128]{2,1,0:T(8,128)} %leaf_pivot.1, s32[2,128]{1,0:T(2,128)} %signs.1, f32[2,128]{1,0:T(2,128)} %perturb.1, ...), custom_call_target="tpu_custom_call" | custom-call | tf_op jit(solution)/shard_map/pallas_call | solution.py:814
  85.0 2.5 %shard_map.131 = (f32[2,128,128]{2,1,0:T(8,128)}, f32[256,256]{1,0:T(8,128)}, f32[512,512]{1,0:T(8,128)}) custom-call(f32[2,128,128]{2,1,0:T(8,128)} %get-tuple-element.6.factor_in, f32[256,256]{1,0:T(8,128)} %get-tuple-element.7.mid_factor_in, f32[512,512]{1,0:T(8,128)} %get-tuple-element.8.upper_in), custom_call_target="tpu_custom_call" | custom-call | tf_op jit(solution)/shard_map/pallas_call | solution.py:877

commit v3 on v2

--- a/solution.py
+++ b/solution.py
@@ -110,6 +110,7 @@
     er,
     xs,
     xr,
+    ts,
     vs,
     vr,
     ks,
@@ -283,6 +284,8 @@
     def edge_pivot_on():
         return edge(piv.at[1], piv.at[1], 2, 1, core_peer)
 
+    rho_y = rho + 1 - 2 * high
+
     def relay_copy():
         return pltpu.make_async_remote_copy(
             src_ref=rbuf.at[whole_u],
@@ -299,25 +302,40 @@
             dst_ref=rbuf.at[col_u],
             send_sem=xs.at[0],
             recv_sem=er.at[0],
-            device_id=(cube, 2),
-            device_id_type=MESH,
-        )
-
-    relays = (front == 0) & (rho == 2)
-    relays_on = (front == 0) & (rho == 3)
+            device_id=(cube, rho_y),
+            device_id_type=MESH,
+        )
+
+    def pivot_on(there):
+        return pltpu.make_async_remote_copy(
+            src_ref=piv.at[1],
+            dst_ref=piv.at[1],
+            send_sem=ts.at[there],
+            recv_sem=er.at[1],
+            device_id=(cube, there),
+            device_id_type=MESH,
+        )
+
+    relays = (front == 0) & (rho != 0)
+    relays_on = (front == 0) & (rho_y != 0)
+    pivots_on = (front == 0) & (rho_y == 0)
 
     def start_edges():
         @pl.when(rho == 0)
         def _():
             edge_pivot(0, core_peer).start()
-            edge_pivot(1, y_peer).start()
+
+            @pl.when(front == 0)
+            def _():
+                edge_pivot(1, y_peer).start()
+
             piv[1] = rbuf[pivot_u, :]
 
         @pl.when(holds_u)
         def _():
             edge_col(0, core_peer).start()
 
-            @pl.when(front != 2)
+            @pl.when(front == 0)
             def _():
                 edge_col(1, y_peer).start()
 
@@ -345,6 +363,13 @@
     @pl.when(relays)
     def _():
         relay_copy().start()
+
+    @pl.when(pivots_on)
+    def _():
+        edge_pivot(0, core_peer).wait_recv()
+        edge_pivot_on().start()
+        for there in (2, 1, 3):
+            pivot_on(there).start()
 
     own_rows = pl.ds(pl.multiple_of(pos_z * SLOTS, 8), SLOTS)
     r1[own_rows, :] = s1[own_rows, :]
@@ -658,9 +683,7 @@
 
     lax.fori_loop(0, 2, lambda turn, carry: gather_group(2 * turn, carry), 0)
 
-    rho_y = rho + 1 - 2 * high
-
-    @pl.when(rho_y == 0)
+    @pl.when((rho_y == 0) & (front != 0))
     def _():
         edge_pivot(0, core_peer).wait_recv()
         edge_pivot_on().start()
@@ -745,7 +768,10 @@
     @pl.when(rho == 0)
     def _():
         edge_pivot(0, core_peer).wait_send()
-        edge_pivot(1, y_peer).wait_send()
+
+        @pl.when(front == 0)
+        def _():
+            edge_pivot(1, y_peer).wait_send()
 
     @pl.when(rho_y == 0)
     def _():
@@ -755,7 +781,7 @@
     def _():
         edge_col(0, core_peer).wait_send()
 
-        @pl.when(front != 2)
+        @pl.when(front == 0)
         def _():
             edge_col(1, y_peer).wait_send()
 
@@ -766,6 +792,11 @@
     @pl.when(relays_on)
     def _():
         relay_on().wait_send()
+
+    @pl.when(pivots_on)
+    def _():
+        for there in (1, 2, 3):
+            pivot_on(there).wait_send()
 
     @pl.when(rho_y == front)
     def _():
@@ -853,6 +884,7 @@
             dma((2,)),
             dma((1,)),
             dma((1,)),
+            dma((4,)),
             dma((2,)),
             dma((2,)),
             dma((15,)),

time: 87.7 us -> 83.2 us (0.949)
  Pallas kernels: 86.8 us -> 82.1 us
    pallas_call x1, Pallas kernels: 84.4 us -> 79.6 us  [local(): pl.pallas_call(functools.partial(fused, depth_z), out_shape=results, in_s...]
where the time goes in v3:
time: 83.2 us; the launch traced here: 82.8 us
  Pallas kernels  82.1 us (99%)
    pallas_call x1, Pallas kernels, local(): pl.pallas_call(functools.partial(fused, depth_z), out_shape=results, in_s...  79.6 us
    pallas_call x1, Pallas kernels, local(): pl.pallas_call(hand_out, out_shape=results, in_specs=[vmem] * 3, out_spec...  2.49 us

profile of v3, /device:TPU:12, one launch (start us, length us, event | category | flops | bytes accessed | tf_op | source)
XLA Modules:
  0.0 82.8 jit_solution(5471218630332750159)
XLA Ops:
  0.6 79.6 %shard_map.130 = (f32[2,128,128]{2,1,0:T(8,128)}, f32[256,256]{1,0:T(8,128)}, f32[512,512]{1,0:T(8,128)}) custom-call(f32[1,256,128]{2,1,0:T(8,128)} %blocks.1, s32[1,256]{1,0:T(1,128)} %bitcast.1, s32[1,256]{1,0:T(1,128)} %target.1, f32[2,128,128]{2,1,0:T(8,128)} %leaf_pivot.1, s32[2,128]{1,0:T(2,128)} %signs.1, f32[2,128]{1,0:T(2,128)} %perturb.1, ...), custom_call_target="tpu_custom_call" | custom-call | tf_op jit(solution)/shard_map/pallas_call | solution.py:845
  80.3 2.5 %shard_map.131 = (f32[2,128,128]{2,1,0:T(8,128)}, f32[256,256]{1,0:T(8,128)}, f32[512,512]{1,0:T(8,128)}) custom-call(f32[2,128,128]{2,1,0:T(8,128)} %get-tuple-element.6.factor_in, f32[256,256]{1,0:T(8,128)} %get-tuple-element.7.mid_factor_in, f32[512,512]{1,0:T(8,128)} %get-tuple-element.8.upper_in), custom_call_target="tpu_custom_call" | custom-call | tf_op jit(solution)/shard_map/pallas_call | solution.py:909

commit v4 on v3

--- a/solution.py
+++ b/solution.py
@@ -355,9 +355,10 @@
             return carry
 
         lax.fori_loop(0, 2 * HALF, push_core, 0)
-        for half in range(2):
-            upper_copy(half, 1, 2 * half).start()
-            upper_copy(half, 3, 2 * half + 1).start()
+        upper_copy(0, 1, 0).start()
+        upper_copy(1, 3, 3).start()
+        upper_copy(1, 1, 2).start()
+        upper_copy(0, 3, 1).start()
         start_edges()
 
     @pl.when(relays)
@@ -469,6 +470,20 @@
         inv_sets[number, 1] = second
         inv_sets[number, 2] = rows_two
         return carry
+
+    @pl.when((front == 1) | (front == 3))
+    def _():
+        half_one = pl.ds(pl.multiple_of(1536 + 128 * (front - 1), 256), 256)
+        passed = pltpu.make_async_remote_copy(
+            src_ref=rbuf.at[half_one],
+            dst_ref=rbuf.at[half_one],
+            send_sem=us.at[0],
+            recv_sem=ur.at[(front - 1) // 2],
+            device_id=(cube, 2),
+            device_id_type=MESH,
+        )
+        passed.wait_recv()
+        passed.start()
 
     def wait_d(step, carry):
         d_copy(step).wait_recv()
@@ -620,20 +635,6 @@
         v_copy(0).start()
 
     v_copy(1).start()
-    @pl.when((front == 1) | (front == 3))
-    def _():
-        half_one = pl.ds(pl.multiple_of(1536 + 128 * (front - 1), 256), 256)
-        passed = pltpu.make_async_remote_copy(
-            src_ref=rbuf.at[half_one],
-            dst_ref=rbuf.at[half_one],
-            send_sem=us.at[0],
-            recv_sem=ur.at[(front - 1) // 2],
-            device_id=(cube, 2),
-            device_id_type=MESH,
-        )
-        passed.wait_recv()
-        passed.start()
-
     @pl.when((front == 1) | (front == 3))
     def _():
         upper_copy(1 - (front - 1) // 2, 1, 0).wait_recv()

time: 83.2 us -> 80.8 us (0.971)
  the two profiles are of different devices: /device:TPU:12 before, /device:TPU:28 now
where the time goes in v4:
time: 80.8 us; the launch traced here: 80.6 us
  Pallas kernels  79.9 us (99%)
    pallas_call x1, Pallas kernels, local(): pl.pallas_call(functools.partial(fused, depth_z), out_shape=results, in_s...  77.4 us
    pallas_call x1, Pallas kernels, local(): pl.pallas_call(hand_out, out_shape=results, in_specs=[vmem] * 3, out_spec...  2.49 us

profile of v4, /device:TPU:28, one launch (start us, length us, event | category | flops | bytes accessed | tf_op | source)
XLA Modules:
  0.0 80.6 jit_solution(9175100602843672296)
XLA Ops:
  0.6 77.4 %shard_map.130 = (f32[2,128,128]{2,1,0:T(8,128)}, f32[256,256]{1,0:T(8,128)}, f32[512,512]{1,0:T(8,128)}) custom-call(f32[1,256,128]{2,1,0:T(8,128)} %blocks.1, s32[1,256]{1,0:T(1,128)} %bitcast.1, s32[1,256]{1,0:T(1,128)} %target.1, f32[2,128,128]{2,1,0:T(8,128)} %leaf_pivot.1, s32[2,128]{1,0:T(2,128)} %signs.1, f32[2,128]{1,0:T(2,128)} %perturb.1, ...), custom_call_target="tpu_custom_call" | custom-call | tf_op jit(solution)/shard_map/pallas_call | solution.py:846
  78.1 2.5 %shard_map.131 = (f32[2,128,128]{2,1,0:T(8,128)}, f32[256,256]{1,0:T(8,128)}, f32[512,512]{1,0:T(8,128)}) custom-call(f32[2,128,128]{2,1,0:T(8,128)} %get-tuple-element.6.factor_in, f32[256,256]{1,0:T(8,128)} %get-tuple-element.7.mid_factor_in, f32[512,512]{1,0:T(8,128)} %get-tuple-element.8.upper_in), custom_call_target="tpu_custom_call" | custom-call | tf_op jit(solution)/shard_map/pallas_call | solution.py:910
